TPU v7x, 32 devices: a whole 2x2x4 slice. The times are simulated.
32 devices in a mesh: enc: 2 (over x), batch: 16 (over z, y, core).
Axes of the slice: x: 2, y: 2, z: 4, core: 2. Of those that a mesh axis runs over, the one named last changes fastest.
Arguments:
- tokens: bfloat16 [2, 16384, 768], P('enc', 'batch'), may hold values from -6 to 6
- cotangent: bfloat16 [2, 16384, 768], P('enc', 'batch'), may hold values from -6 to 6
- projection: bfloat16 [2, 768, 2304], P('enc'), may hold values from -0.21875 to 0.21875
- offsets: bfloat16 [2, 1536], P('enc'), may hold values from -1.1953125 to 1.1953125
- merger: bfloat16 [2, 768, 768], P('enc'), may hold values from -1.75 to 1.75
- adjust: bfloat16 [2, 768], P('enc'), may hold values from -1.1953125 to 1.1953125
- scaling: bfloat16 [2, 768], P('enc'), may hold values from 0.5 to 1.5
- centering: bfloat16 [2, 768], P('enc'), may hold values from -1.1953125 to 1.1953125
- expansion: bfloat16 [2, 768, 3072], P('enc'), may hold values from -0.21875 to 0.21875
- lifting: bfloat16 [2, 3072], P('enc'), may hold values from -1.1953125 to 1.1953125
- contraction: bfloat16 [2, 3072, 768], P('enc'), may hold values from -0.15625 to 0.15625
- settling: bfloat16 [2, 768], P('enc'), may hold values from -1.1953125 to 1.1953125
- rescale: bfloat16 [2, 768], P('enc'), may hold values from 0.5 to 1.5
- recenter: bfloat16 [2, 768], P('enc'), may hold values from -1.1953125 to 1.1953125
- segments: int32 [16384], P('batch'), may hold values from 0 to 15, as said below
- passage_starts: int32 [256], P('batch'), may hold values from 0 to 1023, as said below
- passage_counts: int32 [16], replicated, may hold values from 4 to 16, as said below
- positives: int32 [256], P('batch'), may hold values from 0 to 255, as said below
Outputs:
- encoded: bfloat16 [2, 16384, 768], P('enc', 'batch')
- tokens_gradient: float32 [2, 16384, 768], P('enc', 'batch')
- gradient_projection: float32 [2, 768, 2304], P('enc')
- gradient_offsets: float32 [2, 1536], P('enc')
- gradient_merger: float32 [2, 768, 768], P('enc')
- gradient_adjust: float32 [2, 768], P('enc')
- gradient_scaling: float32 [2, 768], P('enc')
- gradient_centering: float32 [2, 768], P('enc')
- gradient_expansion: float32 [2, 768, 3072], P('enc')
- gradient_lifting: float32 [2, 3072], P('enc')
- gradient_contraction: float32 [2, 3072, 768], P('enc')
- gradient_settling: float32 [2, 768], P('enc')
- gradient_rescale: float32 [2, 768], P('enc')
- gradient_recenter: float32 [2, 768], P('enc')
Inputs may be any that keep to these rules, and one draw needn't show every extreme that they name: `segments`: within one index of batch, passages are runs of consecutive tokens numbered from 0 upward in order; every row of 256 tokens starts a passage and holds 1 to 4 of them; passages start at multiples of 8. `passage_starts`: on each index of batch, slot s below that index's passage count holds the position of passage s's first token; other slots hold arbitrary positions. `passage_counts`: the number of passages on each index of batch; some index holds 16 in every draw. `positives`: A slot i * 16 + s with s below the passage count of index i.
All inputs are finite; a program needn't handle non-finite values.
Results may differ from a plain program's by a relative error of at most 0.014.
Values may be sent and summed in bfloat16 or wider, within the bound.
No kernel may reach another device: no remote copies, remote signals or barrier semaphores. Data moves between devices by JAX's collectives and lax.ppermute only.
A program may use at most 192 MiB of HBM per device.

v0:
```python
import math
import jax
import jax.numpy as jnp
from jax import lax
from jax.sharding import PartitionSpec as P

HEADS = 12
QLEN = 64
BLOCK = 512
EPSILON = 1e-12
SHARPNESS_DIVISOR = 2.0
LOSS_WEIGHT = 2.0
FLOAT_KIND = jnp.float32
BRAIN = jnp.bfloat16


def swapped(value, axis, apart):
    mask = 2**apart
    pairs = [(source, source ^ mask) for source in range(lax.axis_size(axis))]
    return lax.ppermute(value, axis, pairs)


def layer_norm(values, scale_row, shift_row):
    centered = values - jnp.mean(values, axis=-1, keepdims=True)
    spread = jnp.mean(centered * centered, axis=-1, keepdims=True)
    return centered * lax.rsqrt(spread + EPSILON) * scale_row + shift_row


def exact_gelu(values):
    return jax.nn.gelu(values, approximate=False)


def to_low(values):
    return values.astype(BRAIN)


def block_scores(queries, key_rows, block_marks):
    score_scale = 1.0 / math.sqrt(queries.shape[2])
    scores = (
        jnp.einsum("qhd,khd->hqk", queries, key_rows, preferred_element_type=FLOAT_KIND)
        * score_scale
    )
    same_mark = block_marks[:, None] == block_marks[None, :]
    return jnp.where(same_mark[None], scores, -1e30)


def attend_forward(parts):
    queries, key_rows, values, block_marks = parts
    scores = block_scores(queries, key_rows, block_marks)
    row_top = jnp.max(scores, axis=-1, keepdims=True)
    log_total = row_top + jnp.log(jnp.sum(jnp.exp(scores - row_top), axis=-1, keepdims=True))
    weights = to_low(jnp.exp(scores - log_total))
    context = jnp.einsum("hqk,khd->qhd", weights, values, preferred_element_type=FLOAT_KIND)
    return (to_low(context), log_total)


def attend_backward(parts):
    queries, key_rows, values, block_marks, log_total, gradient_context = parts
    score_scale = 1.0 / math.sqrt(queries.shape[2])
    probability = jnp.exp(block_scores(queries, key_rows, block_marks) - log_total)
    gradient_values = jnp.einsum(
        "hqk,qhd->khd", to_low(probability), gradient_context, preferred_element_type=FLOAT_KIND
    )
    gradient_probs = jnp.einsum(
        "qhd,khd->hqk", gradient_context, values, preferred_element_type=FLOAT_KIND
    )
    row_dots = jnp.sum(probability * gradient_probs, axis=-1, keepdims=True)
    gradient_scores = to_low(probability * (gradient_probs - row_dots))
    gradient_queries = (
        jnp.einsum("hqk,khd->qhd", gradient_scores, key_rows, preferred_element_type=FLOAT_KIND)
        * score_scale
    )
    gradient_keys = (
        jnp.einsum("hqk,qhd->khd", gradient_scores, queries, preferred_element_type=FLOAT_KIND)
        * score_scale
    )
    return (gradient_queries, gradient_keys, gradient_values)


def column_sums(values):
    return jnp.sum(values.astype(FLOAT_KIND), axis=0)


def logit_gradients(
    question_row_block, target_row_list, passage_row_block, valid_entries, smoothing_divisor
):
    score_matrix = (
        jnp.einsum(
            "qd,sd->qs", question_row_block, passage_row_block, preferred_element_type=FLOAT_KIND
        )
        * smoothing_divisor
    )
    score_matrix = jnp.where(valid_entries[None, :], score_matrix, -1e30)
    row_top = jnp.max(score_matrix, axis=1, keepdims=True)
    logit_total = row_top + jnp.log(jnp.sum(jnp.exp(score_matrix - row_top), axis=1, keepdims=True))
    probability = jnp.exp(score_matrix - logit_total)
    target_hit = (
        jnp.arange(score_matrix.shape[1], dtype=jnp.int32)[None, :] == target_row_list[:, None]
    )
    return to_low(LOSS_WEIGHT * (probability - target_hit.astype(FLOAT_KIND)))


def shards(
    tokens,
    cotangent,
    projection,
    offsets,
    merger,
    adjust,
    scaling,
    centering,
    expansion,
    lifting,
    contraction,
    settling,
    rescale,
    recenter,
    segments,
    passage_starts,
    passage_counts,
    positives,
):
    enc_index = lax.axis_index("enc")
    is_passage = enc_index == 1
    rows_in = tokens[0]
    row_count, feature_breadth = rows_in.shape
    head_count = HEADS
    head_size = feature_breadth // head_count
    block_count = row_count // BLOCK
    focus_weighting_array = projection[0]
    merge_matrix = merger[0]
    expand_matrix = expansion[0]
    shrink_matrix = contraction[0]
    offset_row = offsets[0].astype(FLOAT_KIND)
    adjust_row = adjust[0].astype(FLOAT_KIND)
    scaling_row = scaling[0].astype(FLOAT_KIND)
    centering_row = centering[0].astype(FLOAT_KIND)
    lifting_row = lifting[0].astype(FLOAT_KIND)
    settling_row = settling[0].astype(FLOAT_KIND)
    rescale_row = rescale[0].astype(FLOAT_KIND)
    recenter_row = recenter[0].astype(FLOAT_KIND)
    position = jnp.arange(row_count, dtype=jnp.int32)
    token_marks = jnp.where(is_passage, segments, position // QLEN)
    block_marks = token_marks.reshape(block_count, BLOCK)
    full_bias = jnp.concatenate(
        [
            offset_row[:feature_breadth],
            jnp.zeros((feature_breadth,), FLOAT_KIND),
            offset_row[feature_breadth:],
        ]
    )
    packed = to_low(
        jnp.dot(rows_in, focus_weighting_array, preferred_element_type=FLOAT_KIND) + full_bias
    )
    parted = packed.reshape(block_count, BLOCK, 3, head_count, head_size)
    queries = parted[:, :, 0]
    key_rows = parted[:, :, 1]
    values = parted[:, :, 2]
    context, log_total = lax.map(attend_forward, (queries, key_rows, values, block_marks))
    context = context.reshape(row_count, feature_breadth)
    attended = jnp.dot(context, merge_matrix, preferred_element_type=FLOAT_KIND) + adjust_row
    normed_one, first_back = jax.vjp(
        layer_norm, rows_in.astype(FLOAT_KIND) + attended, scaling_row, centering_row
    )
    first_low = to_low(normed_one)
    hidden = jnp.dot(first_low, expand_matrix, preferred_element_type=FLOAT_KIND) + lifting_row
    activated = to_low(exact_gelu(hidden))
    shrunk = jnp.dot(activated, shrink_matrix, preferred_element_type=FLOAT_KIND) + settling_row
    encoded, second_back = jax.vjp(layer_norm, normed_one + shrunk, rescale_row, recenter_row)
    encoded_low = to_low(encoded)
    slot_count = passage_starts.shape[0]
    half_count = slot_count // 2
    slot_index = jnp.arange(slot_count, dtype=jnp.int32)
    summary_rows = jnp.where(is_passage, passage_starts, slot_index * QLEN)
    picker = summary_rows[:, None] == position[None, :]
    summary_local = to_low(
        jnp.dot(picker.astype(BRAIN), encoded_low, preferred_element_type=FLOAT_KIND)
    )
    partner = swapped(summary_local, "enc", 0)
    passage_embedding = jnp.where(is_passage, summary_local, partner)
    question_embedding = jnp.where(is_passage, partner, summary_local)
    smoothing_divisor = SHARPNESS_DIVISOR / math.sqrt(feature_breadth)
    valid_entries = (slot_index[None, :] < passage_counts[:, None]).reshape(-1)
    collected_rows = lax.all_gather(passage_embedding, "batch", axis=0, tiled=True)
    local_questions = lax.dynamic_slice_in_dim(
        question_embedding, enc_index * half_count, half_count, 0
    )
    local_targets = lax.dynamic_slice_in_dim(positives, enc_index * half_count, half_count, 0)
    logits_gradient = logit_gradients(
        local_questions, local_targets, collected_rows, valid_entries, smoothing_divisor
    )
    gradient_questions = (
        jnp.dot(logits_gradient, collected_rows, preferred_element_type=FLOAT_KIND)
        * smoothing_divisor
    )
    gradient_passages = lax.psum_scatter(
        jnp.einsum("qs,qd->sd", logits_gradient, local_questions, preferred_element_type=FLOAT_KIND)
        * smoothing_divisor,
        "batch",
        scatter_dimension=0,
        tiled=True,
    )
    back_questions, back_passages = (
        swapped(gradient_questions.astype(jnp.bfloat16), "enc", 0).astype(gradient_questions.dtype),
        swapped(gradient_passages.astype(jnp.bfloat16), "enc", 0).astype(gradient_passages.dtype),
    )
    gradient_summary = jnp.where(
        is_passage,
        gradient_passages + back_passages,
        jnp.concatenate([gradient_questions, back_questions], axis=0),
    )
    gradient_encoded = cotangent[0].astype(FLOAT_KIND) + jnp.einsum(
        "ct,cd->td", picker.astype(FLOAT_KIND), gradient_summary, precision=lax.Precision.HIGHEST
    )
    gradient_two, gradient_rescale, gradient_recenter = second_back(gradient_encoded)
    gradient_shrunk = to_low(gradient_two)
    gradient_settling = column_sums(gradient_shrunk)
    gradient_contraction = jnp.einsum(
        "tf,td->fd", activated, gradient_shrunk, preferred_element_type=FLOAT_KIND
    )
    gradient_activated = jnp.einsum(
        "td,fd->tf", gradient_shrunk, shrink_matrix, preferred_element_type=FLOAT_KIND
    )
    gelu_again, gelu_back = jax.vjp(exact_gelu, hidden)
    gradient_hidden = to_low(gelu_back(gradient_activated)[0])
    gradient_lifting = column_sums(gradient_hidden)
    gradient_expansion = jnp.einsum(
        "td,tf->df", first_low, gradient_hidden, preferred_element_type=FLOAT_KIND
    )
    gradient_first = gradient_two + jnp.einsum(
        "tf,df->td", gradient_hidden, expand_matrix, preferred_element_type=FLOAT_KIND
    )
    gradient_one, gradient_scaling, gradient_centering = first_back(gradient_first)
    gradient_attended = to_low(gradient_one)
    gradient_adjust = column_sums(gradient_attended)
    gradient_merger = jnp.einsum(
        "tc,td->cd", context, gradient_attended, preferred_element_type=FLOAT_KIND
    )
    gradient_context = to_low(
        jnp.einsum("td,cd->tc", gradient_attended, merge_matrix, preferred_element_type=FLOAT_KIND)
    )
    gradient_context = gradient_context.reshape(block_count, BLOCK, head_count, head_size)
    gradient_queries, gradient_keys, gradient_values = lax.map(
        attend_backward, (queries, key_rows, values, block_marks, log_total, gradient_context)
    )
    gradient_packed = to_low(
        jnp.stack([gradient_queries, gradient_keys, gradient_values], axis=2).reshape(
            row_count, 3 * feature_breadth
        )
    )
    packed_sums = column_sums(gradient_packed)
    gradient_offsets = jnp.concatenate(
        [packed_sums[:feature_breadth], packed_sums[2 * feature_breadth :]]
    )
    gradient_projection = jnp.einsum(
        "td,te->de", rows_in, gradient_packed, preferred_element_type=FLOAT_KIND
    )
    tokens_gradient = gradient_one + jnp.einsum(
        "te,de->td", gradient_packed, focus_weighting_array, preferred_element_type=FLOAT_KIND
    )
    every_share = (
        lax.psum_scatter(gradient_projection, "batch", scatter_dimension=0, tiled=True),
        lax.psum_scatter(gradient_offsets, "batch", scatter_dimension=0, tiled=True),
        lax.psum_scatter(gradient_merger, "batch", scatter_dimension=0, tiled=True),
        lax.psum_scatter(gradient_adjust, "batch", scatter_dimension=0, tiled=True),
        lax.psum_scatter(gradient_scaling, "batch", scatter_dimension=0, tiled=True),
        lax.psum_scatter(gradient_centering, "batch", scatter_dimension=0, tiled=True),
        lax.psum_scatter(gradient_expansion, "batch", scatter_dimension=0, tiled=True),
        lax.psum_scatter(gradient_lifting, "batch", scatter_dimension=0, tiled=True),
        lax.psum_scatter(gradient_contraction, "batch", scatter_dimension=0, tiled=True),
        lax.psum_scatter(gradient_settling, "batch", scatter_dimension=0, tiled=True),
        lax.psum_scatter(gradient_rescale, "batch", scatter_dimension=0, tiled=True),
        lax.psum_scatter(gradient_recenter, "batch", scatter_dimension=0, tiled=True),
    )
    overall_aggregate = (
        lax.all_gather(every_share[0].astype(jnp.bfloat16), "batch", axis=0, tiled=True).astype(
            jnp.float32
        ),
        lax.all_gather(every_share[1].astype(jnp.bfloat16), "batch", axis=0, tiled=True).astype(
            jnp.float32
        ),
        lax.all_gather(every_share[2].astype(jnp.bfloat16), "batch", axis=0, tiled=True).astype(
            jnp.float32
        ),
        lax.all_gather(every_share[3].astype(jnp.bfloat16), "batch", axis=0, tiled=True).astype(
            jnp.float32
        ),
        lax.all_gather(every_share[4].astype(jnp.bfloat16), "batch", axis=0, tiled=True).astype(
            jnp.float32
        ),
        lax.all_gather(every_share[5].astype(jnp.bfloat16), "batch", axis=0, tiled=True).astype(
            jnp.float32
        ),
        lax.all_gather(every_share[6].astype(jnp.bfloat16), "batch", axis=0, tiled=True).astype(
            jnp.float32
        ),
        lax.all_gather(every_share[7].astype(jnp.bfloat16), "batch", axis=0, tiled=True).astype(
            jnp.float32
        ),
        lax.all_gather(every_share[8].astype(jnp.bfloat16), "batch", axis=0, tiled=True).astype(
            jnp.float32
        ),
        lax.all_gather(every_share[9].astype(jnp.bfloat16), "batch", axis=0, tiled=True).astype(
            jnp.float32
        ),
        lax.all_gather(every_share[10].astype(jnp.bfloat16), "batch", axis=0, tiled=True).astype(
            jnp.float32
        ),
        lax.all_gather(every_share[11].astype(jnp.bfloat16), "batch", axis=0, tiled=True).astype(
            jnp.float32
        ),
    )
    attend_total = overall_aggregate[:6]
    expand_total = overall_aggregate[6:]
    return (
        to_low(encoded)[None],
        tokens_gradient[None],
        attend_total[0][None],
        attend_total[1][None],
        attend_total[2][None],
        attend_total[3][None],
        attend_total[4][None],
        attend_total[5][None],
        expand_total[0][None],
        expand_total[1][None],
        expand_total[2][None],
        expand_total[3][None],
        expand_total[4][None],
        expand_total[5][None],
    )


def solution(mesh):
    return jax.shard_map(
        shards,
        mesh=mesh,
        in_specs=(
            P("enc", "batch", None),
            P("enc", "batch", None),
            P("enc", None, None),
            P("enc", None),
            P("enc", None, None),
            P("enc", None),
            P("enc", None),
            P("enc", None),
            P("enc", None, None),
            P("enc", None),
            P("enc", None, None),
            P("enc", None),
            P("enc", None),
            P("enc", None),
            P("batch"),
            P("batch"),
            P(),
            P("batch"),
        ),
        out_specs=(
            P("enc", "batch", None),
            P("enc", "batch", None),
            P("enc", None, None),
            P("enc", None),
            P("enc", None, None),
            P("enc", None),
            P("enc", None),
            P("enc", None),
            P("enc", None, None),
            P("enc", None),
            P("enc", None, None),
            P("enc", None),
            P("enc", None),
            P("enc", None),
        ),
        check_vma=False,
    )
```

profile of v0, /device:TPU:0, one launch (start us, length us, event | category | flops | bytes accessed | tf_op | source)
XLA Modules:
  0.0 909.3 jit_solution(17320595831040693999)
XLA Ops:
  14.7 7.3 add_convert_fusion.1
  22.0 6.6 copy.99
  28.6 8.8 reshape.236
  37.4 5.4 slice_bitcast_fusion
  47.3 26.3 %while.26 = (s32[]{:T(128)}, bf16[2,512,12,64]{1,3,2,0:T(8,128)(2,1)}, f32[2,12,512,1]{2,1,3,0:T(8,128)}, bf16[2,512,12,64]{1,3,2,0:T(8,128)(2,1)}, s32[2,512]{1...) while((s32[]{:T(128)}, ...), condition=%wide.region_3.4_spmd, body=%wide.region_0.3_spmd.sunk | while | flops 840558592 | bytes 43204736 | solution.py:159
  81.7 35.9 %multiply_convert_fusion.1 = (bf16[1024,3072]{1,0:T(8,128)(2,1)}, f32[1024,3072]{1,0:T(8,128)}, f32[1024,3072]{1,0:T(8,128)}) fusion(f32[3072]{0:T(1024)S(1)} %bitcast.227, bf16[1,768,3072]{2,1,0:T(8,128)(2,1)S(1)} %bitcast.233, f32[1024,768]{0,1:T(8,128)S(1)} %get-tuple-element.312, f32[768]{0:T(1024)S(1)} %get-tuple-element.324, ...), kind=kOutput, calls=%fused_computation.63 | convolution fusion | flops 5043388416 | bytes 39348224 | tf_op jit(solution)/shard_map/dot_general | solution.py:166
  117.7 7.7 fusion.99
  135.6 22.7 %all_gather.39 = bf16[256,768]{1,0:T(8,128)(2,1)S(1)} all-gather(bf16[16,768]{1,0:T(8,128)(2,1)S(1)} %broadcast_select_fusion), channel_id=1, replica_groups=mesh['enc'=2,'batch'=16] {'batch'}, dimensions={0}, use_global_device_ids=true | all-gather | bytes 417792 | tf_op jit(solution)/shard_map/all_gather | solution.py:184
  162.9 53.9 %reduce-scatter.8.cloned.1.call-done = f32[16,768]{1,0:T(8,128)} async-done(((f32[256,768]{1,0:T(8,128)}), f32[16,768]{1,0:T(8,128)}) %reduce-scatter.8.cloned.1.call-update) | async-done | bytes 49168 | tf_op jit(solution)/shard_map/reduce_scatter | solution.py:196
  226.3 5.8 multiply_reduce_fusion.1
  235.2 19.2 %convert_reduce_fusion = (f32[3072]{0:T(1024)}, bf16[1024,3072]{1,0:T(8,128)(2,1)}) fusion(f32[1024,3072]{1,0:T(8,128)} %get-tuple-element.299, bf16[1024,768]{0,1:T(8,128)(2,1)} %get-tuple-element.289, bf16[1,3072,768]{2,1,0:T(8,128)(2,1)} %param.32, f32[1024,3072]{1,0:T(8,128)} %get-tuple-element.313, f32[3072]{0:T(1024)S(1)} %bitcast.228), kind=kOutput, calls=%fused_computation.61 | convolution fusion | flops 4885312512 | bytes 37773312 | tf_op jit(solution)/shard_map/td,fd->tf/dot_general | solution.py:221
  254.5 11.0 %multiply_reduce_fusion.2 = (f32[768]{0:T(1024)}, f32[1024]{0:T(1024)S(1)}, f32[768]{0:T(1024)}, f32[1024,768]{0,1:T(8,128)S(1)}) fusion(f32[1024,768]{0,1:T(8,128)S(1)} %copy-done.10, f32[1024]{0:T(1024)S(1)} %copy-done.46, f32[1024]{0:T(1024)S(1)} %copy-done.35, f32[768]{0:T(1024)S(1)} %copy-done.42, bf16[1024,3072]{1,0:T(8,128)(2,1)} %get-tuple-element.323, ...), kind=kOutput, calls=%fused_computation.99 | convolution fusion | flops 4839699456 | bytes 20472832 | tf_op jit(solution)/shard_map/tf,df->td/dot_general | solution.py:230
  286.5 53.6 %while.27 = (s32[]{:T(128)}, bf16[2,512,12,64]{1,3,2,0:T(8,128)(2,1)}, bf16[2,512,12,64]{1,3,2,0:T(8,128)(2,1)}, bf16[2,512,12,64]{1,3,2,0:T(8,128)(2,1)}, bf16[...) while((s32[]{:T(128)}, ...), condition=%wide.region_17.18_spmd, body=%wide.region_15.17_spmd.sunk | while | flops 2061494272 | bytes 156175728 | solution.py:243
  294.9 6.8 multiply_reduce_fusion.8
  301.7 7.3 multiply_convert_fusion.6
  321.7 6.8 multiply_reduce_fusion.8
  328.5 7.2 multiply_convert_fusion.6
  345.1 9.4 %copy.112 = bf16[2,512,3,12,64]{1,0,4,3,2:T(2,128)(2,1)} copy(bf16[2,512,3,12,64]{1,4,3,0,2:T(8,128)(2,1)} %get-tuple-element.293) | data formatting | bytes 9437184 | tf_op jit(solution)/shard_map/stack | solution.py:247
  360.7 5.8 convolution_bitcast_fusion
  366.5 8.0 copy.124
  374.6 9.9 %fusion.103 = f32[3072,768]{1,0:T(8,128)} fusion(bf16[1024,3072]{1,0:T(8,128)(2,1)} %get-tuple-element.298, bf16[1024,768]{0,1:T(8,128)(2,1)} %get-tuple-element.289), kind=kOutput, calls=%fused_computation.197 | convolution fusion | flops 4831838208 | bytes 17301504 | tf_op jit(solution)/shard_map/tf,td->fd/dot_general | solution.py:218
  385.2 11.3 %fusion.90 = f32[768,3072]{1,0:T(8,128)} fusion(bf16[1024,3072]{1,0:T(8,128)(2,1)} %get-tuple-element.323, f32[1024,768]{0,1:T(8,128)} %copy-done.9, f32[768]{0:T(1024)S(1)} %copy-done.55, f32[768]{0:T(1024)S(1)} %copy-done.43, f32[1024]{0:T(1024)S(1)} %copy-done.47, f32[1024]{0:T(1024)S(1)} %copy-done.36), kind=kOutput, calls=%fused_computation.187 | convolution fusion | flops 4835770368 | bytes 18888704 | tf_op jit(solution)/shard_map/td,tf->df/dot_general | solution.py:227
  398.2 65.3 %reduce-scatter.16.cloned.1.call-done = f32[48,2304]{1,0:T(8,128)} async-done(((f32[768,2304]{1,0:T(8,128)}), f32[48,2304]{1,0:T(8,128)}) %reduce-scatter.16.cloned.1.call-update) | async-done | bytes 442384 | tf_op jit(solution)/shard_map/reduce_scatter | solution.py:262
  465.4 114.2 %reduce-scatter.14.cloned.1.call-done = f32[192,768]{1,0:T(8,128)} async-done(((f32[3072,768]{1,0:T(8,128)}), f32[192,768]{1,0:T(8,128)}) %reduce-scatter.14.cloned.1.call-update) | async-done | bytes 589840 | tf_op jit(solution)/shard_map/reduce_scatter | solution.py:270
  581.4 113.7 %reduce-scatter.12.cloned.1.call-done = f32[48,3072]{1,0:T(8,128)} async-done(((f32[768,3072]{1,0:T(8,128)}), f32[48,3072]{1,0:T(8,128)}) %reduce-scatter.12.cloned.1.call-update) | async-done | bytes 589840 | tf_op jit(solution)/shard_map/reduce_scatter | solution.py:268
  710.5 62.2 %all-reduce.16 = (bf16[1536]{0:T(1024)(128)(2,1)}, bf16[768]{0:T(1024)(128)(2,1)}, bf16[768]{0:T(1024)(128)(2,1)}, bf16[768]{0:T(1024)(128)(2,1)}, bf16[768]{0:T...) all-reduce(f32[1536]{0:T(1024)S(1)} %pad_maximum_fusion.2, ...), channel_id=4, replica_groups=mesh['enc'=2,'batch'=16] {'batch'}, use_global_device_ids=true, to_apply=%region_20.21.clone | all-reduce | flops 9216 | bytes 55296
  789.1 58.6 %all-reduce.17 = (bf16[1536]{0:T(1024)(128)(2,1)}, bf16[768]{0:T(1024)(128)(2,1)}, bf16[768]{0:T(1024)(128)(2,1)}, bf16[768]{0:T(1024)(128)(2,1)}, bf16[768]{0:T...) all-reduce(bf16[1536]{0:T(1024)(128)(2,1)S(1)} %dynamic-update-slic, ...), channel_id=1, replica_groups=mesh['enc'=2,'batch'=16] {'batch'}, use_global_device_ids=true, to_apply=%add | all-reduce | flops 9216 | bytes 36864
  857.8 8.0 add_bitcast_fusion
  872.2 5.5 bitcast_convert_fusion.2
  877.7 6.9 bitcast_convert_fusion
  884.6 10.4 %all-gather.9.cloned.1.call-done = bf16[768,3072]{1,0:T(8,128)(2,1)} async-done(((bf16[48,3072]{1,0:T(8,128)(2,1)}), bf16[768,3072]{1,0:T(8,128)(2,1)}) %all-gather.9.cloned.1.call-update) | async-done | bytes 4718608 | tf_op jit(solution)/shard_map/all_gather | solution.py:294
  894.9 7.4 bitcast_convert_fusion.1
  (317 shorter events, 180.8 us)
Async XLA Ops:
  7.2 209.6 %reduce-scatter.8.cloned.1.call-start = ((), (), s32[]{:S(2)}) async-start(), calls=%async_computation.5 | async-start | bytes 835584 | tf_op jit(solution)/shard_map/reduce_scatter | solution.py:196
  77.3 40.4 %slice-start = ((s8[4718592]{0:T(1024)(128)(4,1)}), s8[4194304]{0:T(1024)(128)(4,1)S(1)}, s32[]{:S(2)}) async-start(s8[4718592]{0:T(1024)(128)(4,1)} %bitcast.230), calls=%async_computation.14 | async-start | bytes 8388608
  79.0 38.7 %copy-start.9 = (f32[1024,768]{0,1:T(8,128)}, f32[1024,768]{0,1:T(8,128)S(1)}, u32[]{:S(2)}) copy-start(f32[1024,768]{0,1:T(8,128)S(1)} %get-tuple-element.312) | copy-start | bytes 9437188
  79.0 38.6 %copy-start.34 = (f32[1024]{0:T(1024)}, f32[1024]{0:T(1024)S(1)}, u32[]{:S(2)}) copy-start(f32[1024]{0:T(1024)S(1)} %broadcast_multiply_fusion.1) | copy-start | bytes 12292
  81.6 36.1 %copy-start.45 = (f32[1024]{0:T(1024)}, f32[1024]{0:T(1024)S(1)}, u32[]{:S(2)}) copy-start(f32[1024]{0:T(1024)S(1)} %fusion.85) | copy-start | bytes 12292
  81.6 36.0 %copy-start.41 = (f32[768]{0:T(1024)}, f32[768]{0:T(1024)S(1)}, u32[]{:S(2)}) copy-start(f32[768]{0:T(1024)S(1)} %get-tuple-element.325) | copy-start | bytes 9220
  81.6 36.0 %copy-start.54 = (f32[768]{0:T(1024)}, f32[768]{0:T(1024)S(1)}, u32[]{:S(2)}) copy-start(f32[768]{0:T(1024)S(1)} %get-tuple-element.324) | copy-start | bytes 9220
  81.7 36.0 %copy-start.56 = (f32[768]{0:T(1024)S(1)}, f32[768]{0:T(1024)}, u32[]{:S(2)}) copy-start(f32[768]{0:T(1024)} %convert_reduce_fusion.6) | copy-start | bytes 9220
  81.7 36.0 %slice-start.1 = ((s8[4718592]{0:T(1024)(128)(4,1)}), s8[524288]{0:T(1024)(128)(4,1)S(1)}, s32[]{:S(2)}) async-start(s8[4718592]{0:T(1024)(128)(4,1)} %bitcast.230), calls=%async_computation.15 | async-start | bytes 1048576
  125.5 106.6 %copy-start.23 = (f32[1024]{0:T(1024)}, f32[1024]{0:T(1024)S(1)}, u32[]{:S(2)}) copy-start(f32[1024]{0:T(1024)S(1)} %broadcast_multiply_fusion) | copy-start | bytes 12292
  126.5 105.6 %copy-start.27 = (f32[1024]{0:T(1024)}, f32[1024]{0:T(1024)S(1)}, u32[]{:S(2)}) copy-start(f32[1024]{0:T(1024)S(1)} %fusion.86) | copy-start | bytes 12292
  127.9 6.9 collective-permute-start
  134.8 25.5 %copy-start.61 = (s32[8]{0:T(128)}, s32[8]{0:T(128)S(1)}, u32[]{:S(2)}) copy-start(s32[8]{0:T(128)S(1)} %dynamic_slice.40) | copy-start | bytes 100
  162.9 233.7 %reduce-scatter.10.cloned.1.call-start = ((), (), s32[]{:S(2)}) async-start(), calls=%async_computation.7 | async-start | bytes 2506752 | tf_op jit(solution)/shard_map/reduce_scatter | solution.py:264
  218.2 8.0 collective-permute-start.1
  221.6 4.0 collective-permute-start.2
  235.2 19.3 %copy-start.10 = (f32[1024,768]{0,1:T(8,128)S(1)}, f32[1024,768]{0,1:T(8,128)}, u32[]{:S(2)}) copy-start(f32[1024,768]{0,1:T(8,128)} %copy-done.9) | copy-start | bytes 9437188
  235.2 19.3 %copy-start.35 = (f32[1024]{0:T(1024)S(1)}, f32[1024]{0:T(1024)}, u32[]{:S(2)}) copy-start(f32[1024]{0:T(1024)} %copy-done.34) | copy-start | bytes 12292
  235.2 19.3 %copy-start.42 = (f32[768]{0:T(1024)S(1)}, f32[768]{0:T(1024)}, u32[]{:S(2)}) copy-start(f32[768]{0:T(1024)} %copy-done.41) | copy-start | bytes 9220
  235.2 19.3 %copy-start.46 = (f32[1024]{0:T(1024)S(1)}, f32[1024]{0:T(1024)}, u32[]{:S(2)}) copy-start(f32[1024]{0:T(1024)} %copy-done.45) | copy-start | bytes 12292
  254.5 11.0 %copy-start.38 = (f32[1024]{0:T(1024)S(1)}, f32[1024]{0:T(1024)}, u32[]{:S(2)}) copy-start(f32[1024]{0:T(1024)} %copy-done.37) | copy-start | bytes 12292
  286.5 177.1 %reduce-scatter.16.cloned.1.call-start = ((), (), s32[]{:S(2)}) async-start(), calls=%async_computation.13 | async-start | bytes 7520256 | tf_op jit(solution)/shard_map/reduce_scatter | solution.py:262
  374.6 205.0 %reduce-scatter.14.cloned.1.call-start = ((), (), s32[]{:S(2)}) async-start(), calls=%async_computation.11 | async-start | bytes 10027008 | tf_op jit(solution)/shard_map/reduce_scatter | solution.py:270
  384.6 310.6 %reduce-scatter.12.cloned.1.call-start = ((), (), s32[]{:S(2)}) async-start(), calls=%async_computation.9 | async-start | bytes 10027008 | tf_op jit(solution)/shard_map/reduce_scatter | solution.py:268
  396.5 305.7 %copy-start.24 = (f32[1024]{0:T(1024)S(1)}, f32[1024]{0:T(1024)}, u32[]{:S(2)}) copy-start(f32[1024]{0:T(1024)} %copy-done.23) | copy-start | bytes 12292
  396.5 305.7 %copy-start.28 = (f32[1024]{0:T(1024)S(1)}, f32[1024]{0:T(1024)}, u32[]{:S(2)}) copy-start(f32[1024]{0:T(1024)} %copy-done.27) | copy-start | bytes 12292
  396.5 305.7 %copy-start.31 = (f32[768]{0:T(1024)S(1)}, f32[768]{0:T(1024)}, u32[]{:S(2)}) copy-start(f32[768]{0:T(1024)} %copy-done.29) | copy-start | bytes 9220
  396.5 305.7 %copy-start.33 = (f32[768]{0:T(1024)S(1)}, f32[768]{0:T(1024)}, u32[]{:S(2)}) copy-start(f32[768]{0:T(1024)} %copy-done.32) | copy-start | bytes 9220
  396.6 472.8 %all-gather.7.cloned.1.call-start = ((), (), s32[]{:S(2)}) async-start(), calls=%async_computation.8 | async-start | bytes 1253376 | tf_op jit(solution)/shard_map/all_gather | solution.py:282
  398.2 474.0 %all-gather.5.cloned.1.call-start = ((), (), s32[]{:S(2)}) async-start(), calls=%async_computation.6 | async-start | bytes 3760128 | tf_op jit(solution)/shard_map/all_gather | solution.py:276
  465.3 412.4 %all-gather.11.cloned.1.call-start = ((), (), s32[]{:S(2)}) async-start(), calls=%async_computation.12 | async-start | bytes 5013504 | tf_op jit(solution)/shard_map/all_gather | solution.py:300
  581.4 313.5 %all-gather.9.cloned.1.call-start = ((), (), s32[]{:S(2)}) async-start(), calls=%async_computation.10 | async-start | bytes 5013504 | tf_op jit(solution)/shard_map/all_gather | solution.py:294
  (59 other events, 192.4 us)
Sparse Core Ops, SparseCore 0:
  163.0 53.7 reduce-scatter.7
  286.6 61.6 reduce-scatter.9
  374.7 88.8 reduce-scatter.15
  468.7 110.8 reduce-scatter.13
  584.1 111.0 reduce-scatter.11
  697.6 38.2 all-gather.6
  738.5 45.9 all-gather.4
  787.0 52.8 all-gather.10
  843.0 51.9 all-gather.8
where the time goes:
time: 920 us; the launch traced here: 909 us
  waiting for transfers between devices  358 us (39%)
  matrix products  189 us (21%)
  blocking collectives  143 us (16%)
  local copies, waits for them, and re-layouts  115 us (12%)
  other arithmetic  77.7 us (8%)
  between operations  19 us (2%)
    unnamed x2, blocking collectives  121 us
    reduce_scatter x1, waiting for transfers between devices, shards(): lax.psum_scatter(gradient_contraction, 'batch', scatter_dimension=0, tile...  114 us
    reduce_scatter x1, waiting for transfers between devices, shards(): lax.psum_scatter(gradient_expansion, 'batch', scatter_dimension=0, tiled=...  114 us
    reduce_scatter x1, waiting for transfers between devices, shards(): lax.psum_scatter(gradient_projection, 'batch', scatter_dimension=0, tiled...  65.3 us
    reduce_scatter x1, waiting for transfers between devices, shards(): lax.psum_scatter(jnp.einsum('qs,qd->sd', logits_gradient, local_questions...  53.9 us
    unnamed x154, local copies, waits for them, and re-layouts  51.5 us
    dot_general x1, matrix products, shards(): jnp.dot(first_low, expand_matrix, preferred_element_type=FLOAT_KIND)  35.9 us
    all_gather x1, blocking collectives, shards(): lax.all_gather(passage_embedding, 'batch', axis=0, tiled=True)  22.7 us
  transfers between devices with their start and end apart: 12, of which 6 were waited for; matrix products, arithmetic and copies ran while one was open for 20% of the time, Pallas kernels for 0%

commit v1 on v0

--- a/solution.py
+++ b/solution.py
@@ -12,6 +12,28 @@
 LOSS_WEIGHT = 2.0
 FLOAT_KIND = jnp.float32
 BRAIN = jnp.bfloat16
+
+
+def in_order(parts, dim):
+    lengths = list(parts.shape[1:])
+    lengths[dim] *= parts.shape[0]
+    return jnp.moveaxis(parts, 0, dim).reshape(lengths)
+
+
+def gather_around(x, axis, dim):
+    size = lax.axis_size(axis)
+    pairs = [(i, (i + 1) % size) for i in range(size)]
+    back = [(b, a) for a, b in pairs]
+    lower, upper = ([], [])
+    for turn in range(size - 1):
+        if turn % 2 == 0:
+            lower.append(lax.ppermute(lower[-1] if lower else x, axis, pairs))
+        else:
+            upper.append(lax.ppermute(upper[-1] if upper else x, axis, back))
+    blocks = jnp.stack([*lower[::-1], x, *upper])
+    shift = lax.axis_index(axis) - len(lower)
+    blocks = blocks[(jnp.arange(size) - shift) % size]
+    return in_order(blocks, dim)
 
 
 def swapped(value, axis, apart):
@@ -181,7 +203,7 @@
     question_embedding = jnp.where(is_passage, partner, summary_local)
     smoothing_divisor = SHARPNESS_DIVISOR / math.sqrt(feature_breadth)
     valid_entries = (slot_index[None, :] < passage_counts[:, None]).reshape(-1)
-    collected_rows = lax.all_gather(passage_embedding, "batch", axis=0, tiled=True)
+    collected_rows = gather_around(passage_embedding, "batch", 0)
     local_questions = lax.dynamic_slice_in_dim(
         question_embedding, enc_index * half_count, half_count, 0
     )

time: 920 us -> 969 us (1.053)
  starting transfers between devices: 6.67 us -> 38.1 us
  local copies, waits for them, and re-layouts: 115 us -> 137 us
  blocking collectives: 143 us -> 121 us
  waiting for transfers between devices: 358 us -> 375 us
    ppermute x0 -> x15, starting transfers between devices: none -> 31.4 us  [the longest x7 31.3 us: gather_around(): upper.append(lax.ppermute(upper[-1] if upper else x, axis, back))]
    all_gather x1 -> x0, blocking collectives: 22.7 us -> none  [shards(): lax.all_gather(passage_embedding, 'batch', axis=0, tiled=True)]
    unnamed x154 -> x183, local copies, waits for them, and re-layouts: 51.5 us -> 70.4 us
    ppermute x0 -> x15, waiting for transfers between devices: none -> 14.9 us  [the longest x8 14.3 us: gather_around(): lower.append(lax.ppermute(lower[-1] if lower else x, axis, pairs))]
  transfers between devices with their start and end apart: 12 -> 27, of which waited for: 6 -> 17; matrix products, arithmetic and copies ran while one was open for 20% -> 21% of each run, Pallas kernels for 0% -> 0%
where the time goes in v1:
time: 969 us; the launch traced here: 958 us
  waiting for transfers between devices  375 us (39%)
  matrix products  189 us (20%)
  local copies, waits for them, and re-layouts  137 us (14%)
  blocking collectives  121 us (12%)
  other arithmetic  77.6 us (8%)
  starting transfers between devices  38.1 us (4%)
  between operations  19.1 us (2%)
    unnamed x2, blocking collectives  121 us
    reduce_scatter x1, waiting for transfers between devices, shards(): lax.psum_scatter(gradient_contraction, 'batch', scatter_dimension=0, tile...  114 us
    reduce_scatter x1, waiting for transfers between devices, shards(): lax.psum_scatter(gradient_expansion, 'batch', scatter_dimension=0, tiled=...  114 us
    unnamed x183, local copies, waits for them, and re-layouts  70.4 us
    reduce_scatter x1, waiting for transfers between devices, shards(): lax.psum_scatter(gradient_projection, 'batch', scatter_dimension=0, tiled...  64.9 us
    reduce_scatter x1, waiting for transfers between devices, shards(): lax.psum_scatter(jnp.einsum('qs,qd->sd', logits_gradient, local_questions...  54.4 us
    dot_general x1, matrix products, shards(): jnp.dot(first_low, expand_matrix, preferred_element_type=FLOAT_KIND)  35.9 us
    ppermute x7, starting transfers between devices, gather_around(): upper.append(lax.ppermute(upper[-1] if upper else x, axis, back))  31.3 us
  transfers between devices with their start and end apart: 27, of which 17 were waited for; matrix products, arithmetic and copies ran while one was open for 21% of the time, Pallas kernels for 0%

profile of v1, /device:TPU:0, one launch (start us, length us, event | category | flops | bytes accessed | tf_op | source)
XLA Modules:
  0.0 957.6 jit_solution(12947716319518690231)
XLA Ops:
  14.7 7.3 add_convert_fusion.1
  22.0 6.6 copy.99
  28.6 8.8 reshape.288
  37.4 5.4 slice_bitcast_fusion
  47.2 26.3 %while.26 = (s32[]{:T(128)}, bf16[2,512,12,64]{1,3,2,0:T(8,128)(2,1)}, f32[2,12,512,1]{2,1,3,0:T(8,128)}, bf16[2,512,12,64]{1,3,2,0:T(8,128)(2,1)}, s32[2,512]{1...) while((s32[]{:T(128)}, ...), condition=%wide.region_3.4_spmd, body=%wide.region_0.3_spmd.sunk | while | flops 840558592 | bytes 43204736 | solution.py:181
  81.7 35.9 %multiply_convert_fusion.1 = (bf16[1024,3072]{1,0:T(8,128)(2,1)}, f32[1024,3072]{1,0:T(8,128)}, f32[1024,3072]{1,0:T(8,128)}) fusion(f32[3072]{0:T(1024)S(1)} %bitcast.264, bf16[1,768,3072]{2,1,0:T(8,128)(2,1)S(1)} %bitcast.270, f32[1024,768]{0,1:T(8,128)S(1)} %get-tuple-element.312, f32[768]{0:T(1024)S(1)} %get-tuple-element.324, ...), kind=kOutput, calls=%fused_computation.64 | convolution fusion | flops 5043388416 | bytes 39348224 | tf_op jit(solution)/shard_map/dot_general | solution.py:188
  117.7 8.1 fusion.101
  133.9 5.9 collective-permute-done.1
  211.4 54.4 %reduce-scatter.8.cloned.1.call-done = f32[16,768]{1,0:T(8,128)} async-done(((f32[256,768]{1,0:T(8,128)}), f32[16,768]{1,0:T(8,128)}) %reduce-scatter.8.cloned.1.call-update) | async-done | bytes 49168 | tf_op jit(solution)/shard_map/reduce_scatter | solution.py:218
  275.3 5.8 multiply_reduce_fusion.1
  284.2 19.1 %convert_reduce_fusion = (f32[3072]{0:T(1024)}, bf16[1024,3072]{1,0:T(8,128)(2,1)}) fusion(f32[1024,3072]{1,0:T(8,128)} %get-tuple-element.299, bf16[1024,768]{0,1:T(8,128)(2,1)} %get-tuple-element.289, bf16[1,3072,768]{2,1,0:T(8,128)(2,1)} %param.32, f32[1024,3072]{1,0:T(8,128)} %get-tuple-element.313, f32[3072]{0:T(1024)S(1)} %bitcast.265), kind=kOutput, calls=%fused_computation.62 | convolution fusion | flops 4885312512 | bytes 37773312 | tf_op jit(solution)/shard_map/td,fd->tf/dot_general | solution.py:243
  303.4 11.0 %multiply_reduce_fusion.2 = (f32[768]{0:T(1024)}, f32[1024]{0:T(1024)S(1)}, f32[768]{0:T(1024)}, f32[1024,768]{0,1:T(8,128)S(1)}) fusion(f32[1024,768]{0,1:T(8,128)S(1)} %copy-done.9, f32[1024]{0:T(1024)S(1)} %copy-done.53, f32[1024]{0:T(1024)S(1)} %copy-done.37, f32[768]{0:T(1024)S(1)} %copy-done.50, bf16[1024,3072]{1,0:T(8,128)(2,1)} %get-tuple-element.323, ...), kind=kOutput, calls=%fused_computation.100 | convolution fusion | flops 4839699456 | bytes 20472832 | tf_op jit(solution)/shard_map/tf,df->td/dot_general | solution.py:252
  335.5 53.4 %while.27 = (s32[]{:T(128)}, bf16[2,512,12,64]{1,3,2,0:T(8,128)(2,1)}, bf16[2,512,12,64]{1,3,2,0:T(8,128)(2,1)}, bf16[2,512,12,64]{1,3,2,0:T(8,128)(2,1)}, bf16[...) while((s32[]{:T(128)}, ...), condition=%wide.region_17.18_spmd, body=%wide.region_15.17_spmd.sunk | while | flops 2061494272 | bytes 156175728 | solution.py:265
  343.8 6.8 multiply_reduce_fusion.8
  350.6 7.2 multiply_convert_fusion.6
  370.5 6.8 multiply_reduce_fusion.8
  377.4 7.1 multiply_convert_fusion.6
  393.9 9.4 copy.112
  409.4 5.8 convolution_bitcast_fusion
  415.3 8.0 copy.124
  423.3 9.9 %fusion.105 = f32[3072,768]{1,0:T(8,128)} fusion(bf16[1024,3072]{1,0:T(8,128)(2,1)} %get-tuple-element.298, bf16[1024,768]{0,1:T(8,128)(2,1)} %get-tuple-element.289), kind=kOutput, calls=%fused_computation.221 | convolution fusion | flops 4831838208 | bytes 17301504 | tf_op jit(solution)/shard_map/tf,td->fd/dot_general | solution.py:240
  434.0 11.3 %fusion.92 = f32[768,3072]{1,0:T(8,128)} fusion(bf16[1024,3072]{1,0:T(8,128)(2,1)} %get-tuple-element.323, f32[1024,768]{0,1:T(8,128)} %copy-done.8, f32[768]{0:T(1024)S(1)} %copy-done.63, f32[768]{0:T(1024)S(1)} %copy-done.51, f32[1024]{0:T(1024)S(1)} %copy-done.54, f32[1024]{0:T(1024)S(1)} %copy-done.38), kind=kOutput, calls=%fused_computation.211 | convolution fusion | flops 4835770368 | bytes 18888704 | tf_op jit(solution)/shard_map/td,tf->df/dot_general | solution.py:249
  447.0 64.9 %reduce-scatter.16.cloned.1.call-done = f32[48,2304]{1,0:T(8,128)} async-done(((f32[768,2304]{1,0:T(8,128)}), f32[48,2304]{1,0:T(8,128)}) %reduce-scatter.16.cloned.1.call-update) | async-done | bytes 442384 | tf_op jit(solution)/shard_map/reduce_scatter | solution.py:284
  513.7 114.2 %reduce-scatter.14.cloned.1.call-done = f32[192,768]{1,0:T(8,128)} async-done(((f32[3072,768]{1,0:T(8,128)}), f32[192,768]{1,0:T(8,128)}) %reduce-scatter.14.cloned.1.call-update) | async-done | bytes 589840 | tf_op jit(solution)/shard_map/reduce_scatter | solution.py:292
  629.8 113.7 %reduce-scatter.12.cloned.1.call-done = f32[48,3072]{1,0:T(8,128)} async-done(((f32[768,3072]{1,0:T(8,128)}), f32[48,3072]{1,0:T(8,128)}) %reduce-scatter.12.cloned.1.call-update) | async-done | bytes 589840 | tf_op jit(solution)/shard_map/reduce_scatter | solution.py:290
  758.8 62.2 %all-reduce.16 = (bf16[1536]{0:T(1024)(128)(2,1)}, bf16[768]{0:T(1024)(128)(2,1)}, bf16[768]{0:T(1024)(128)(2,1)}, bf16[768]{0:T(1024)(128)(2,1)}, bf16[768]{0:T...) all-reduce(f32[1536]{0:T(1024)S(1)} %pad_maximum_fusion.2, ...), channel_id=4, replica_groups=mesh['enc'=2,'batch'=16] {'batch'}, use_global_device_ids=true, to_apply=%region_20.21.clone | all-reduce | flops 9216 | bytes 55296
  837.3 58.6 %all-reduce.17 = (bf16[1536]{0:T(1024)(128)(2,1)}, bf16[768]{0:T(1024)(128)(2,1)}, bf16[768]{0:T(1024)(128)(2,1)}, bf16[768]{0:T(1024)(128)(2,1)}, bf16[768]{0:T...) all-reduce(bf16[1536]{0:T(1024)(128)(2,1)S(1)} %dynamic-update-slic, ...), channel_id=1, replica_groups=mesh['enc'=2,'batch'=16] {'batch'}, use_global_device_ids=true, to_apply=%add | all-reduce | flops 9216 | bytes 36864
  906.1 8.0 add_bitcast_fusion
  920.4 5.5 bitcast_convert_fusion.2
  925.9 6.9 bitcast_convert_fusion
  932.8 10.4 %all-gather.9.cloned.1.call-done = bf16[768,3072]{1,0:T(8,128)(2,1)} async-done(((bf16[48,3072]{1,0:T(8,128)(2,1)}), bf16[768,3072]{1,0:T(8,128)(2,1)}) %all-gather.9.cloned.1.call-update) | async-done | bytes 4718608 | tf_op jit(solution)/shard_map/all_gather | solution.py:316
  943.3 7.4 bitcast_convert_fusion.1
  (379 shorter events, 245.4 us)
Async XLA Ops:
  7.2 258.6 %reduce-scatter.8.cloned.1.call-start = ((), (), s32[]{:S(2)}) async-start(), calls=%async_computation.5 | async-start | bytes 835584 | tf_op jit(solution)/shard_map/reduce_scatter | solution.py:218
  125.9 155.2 %copy-start.23 = (f32[1024]{0:T(1024)}, f32[1024]{0:T(1024)S(1)}, u32[]{:S(2)}) copy-start(f32[1024]{0:T(1024)S(1)} %broadcast_multiply_fusion) | copy-start | bytes 12292
  127.7 6.1 collective-permute-start
  133.8 6.0 collective-permute-start.1
  139.8 5.9 collective-permute-start.2
  139.9 6.0 collective-permute-start.9
  145.8 5.9 collective-permute-start.3
  145.8 6.0 collective-permute-start.10
  151.8 5.9 collective-permute-start.4
  151.8 5.9 collective-permute-start.11
  157.7 6.1 collective-permute-start.5
  157.8 6.6 collective-permute-start.12
  163.8 6.4 collective-permute-start.6
  164.4 6.2 collective-permute-start.13
  170.1 6.3 collective-permute-start.7
  170.6 8.9 collective-permute-start.14
  176.4 7.6 collective-permute-start.8
  179.5 24.6 %collective-permute-start.15 = (bf16[16,768]{1,0:T(8,128)(2,1)}, bf16[16,768]{1,0:T(8,128)(2,1)S(1)}, u32[]{:S(2)}, u32[]{:S(2)}) collective-permute-start(bf16[16,768]{1,0:T(8,128)(2,1)} %collective-permute-done.14), channel_id=1, source_target_pairs={{1,0},{2,1},{3,2},{4,3},{5,4},{6,5},{7,6},{8,7},{9,8},{10,9},{11,1... | collective-permute-start | bytes 73736 | tf_op jit(solution)/shard_map/ppermute | solution.py:32
  211.3 234.0 %reduce-scatter.10.cloned.1.call-start = ((), (), s32[]{:S(2)}) async-start(), calls=%async_computation.7 | async-start | bytes 2506752 | tf_op jit(solution)/shard_map/reduce_scatter | solution.py:286
  267.2 8.1 collective-permute-start.16
  270.6 4.0 collective-permute-start.17
  335.4 176.5 %reduce-scatter.16.cloned.1.call-start = ((), (), s32[]{:S(2)}) async-start(), calls=%async_computation.13 | async-start | bytes 7520256 | tf_op jit(solution)/shard_map/reduce_scatter | solution.py:284
  423.3 204.6 %reduce-scatter.14.cloned.1.call-start = ((), (), s32[]{:S(2)}) async-start(), calls=%async_computation.11 | async-start | bytes 10027008 | tf_op jit(solution)/shard_map/reduce_scatter | solution.py:292
  433.3 310.2 %reduce-scatter.12.cloned.1.call-start = ((), (), s32[]{:S(2)}) async-start(), calls=%async_computation.9 | async-start | bytes 10027008 | tf_op jit(solution)/shard_map/reduce_scatter | solution.py:290
  445.3 305.3 %copy-start.24 = (f32[1024]{0:T(1024)S(1)}, f32[1024]{0:T(1024)}, u32[]{:S(2)}) copy-start(f32[1024]{0:T(1024)} %copy-done.23) | copy-start | bytes 12292
  445.3 305.3 %copy-start.28 = (f32[1024]{0:T(1024)S(1)}, f32[1024]{0:T(1024)}, u32[]{:S(2)}) copy-start(f32[1024]{0:T(1024)} %copy-done.27) | copy-start | bytes 12292
  445.3 305.3 %copy-start.31 = (f32[768]{0:T(1024)S(1)}, f32[768]{0:T(1024)}, u32[]{:S(2)}) copy-start(f32[768]{0:T(1024)} %copy-done.29) | copy-start | bytes 9220
  445.3 305.3 %copy-start.35 = (f32[768]{0:T(1024)S(1)}, f32[768]{0:T(1024)}, u32[]{:S(2)}) copy-start(f32[768]{0:T(1024)} %copy-done.34) | copy-start | bytes 9220
  445.3 472.3 %all-gather.7.cloned.1.call-start = ((), (), s32[]{:S(2)}) async-start(), calls=%async_computation.8 | async-start | bytes 1253376 | tf_op jit(solution)/shard_map/all_gather | solution.py:304
  447.0 473.5 %all-gather.5.cloned.1.call-start = ((), (), s32[]{:S(2)}) async-start(), calls=%async_computation.6 | async-start | bytes 3760128 | tf_op jit(solution)/shard_map/all_gather | solution.py:298
  513.7 412.3 %all-gather.11.cloned.1.call-start = ((), (), s32[]{:S(2)}) async-start(), calls=%async_computation.12 | async-start | bytes 5013504 | tf_op jit(solution)/shard_map/all_gather | solution.py:322
  629.7 313.5 %all-gather.9.cloned.1.call-start = ((), (), s32[]{:S(2)}) async-start(), calls=%async_computation.10 | async-start | bytes 5013504 | tf_op jit(solution)/shard_map/all_gather | solution.py:316
  (81 other events, 965.7 us)
Sparse Core Ops, SparseCore 0:
  211.5 54.2 reduce-scatter.7
  335.5 61.0 reduce-scatter.9
  423.4 88.4 reduce-scatter.15
  517.0 110.8 reduce-scatter.13
  632.4 111.0 reduce-scatter.11
  745.9 38.3 all-gather.6
  786.8 45.9 all-gather.4
  835.3 52.7 all-gather.10
  891.2 52.0 all-gather.8
